TPU v7x, 128 devices: a whole 4x4x4 slice. The times are simulated.
128 devices in a mesh: dom: 16 (over y, z), grp: 8 (over x, core).
Axes of the slice: x: 4, y: 4, z: 4, core: 2. Of those that a mesh axis runs over, the one named last changes fastest.
Arguments:
- a_strips: bfloat16 [4096, 64, 448], P(('dom', 'grp')), may hold values from -0.25 to 0.25
- p_strips: bfloat16 [4096, 64, 256], P(('dom', 'grp')), may hold values from -1.1953125 to 1.1953125
- nbr_local: int32 [4096, 7], P(('dom', 'grp')), may hold values from 0 to 79, as said below
- ap_slot: int32 [4096, 7, 4], P(('dom', 'grp')), may hold values from 0 to 7, as said below
- tile_slot: int32 [4096, 4, 8], P(('dom', 'grp')), may hold values from 0 to 71, as said below
- send_rows: int32 [128, 8, 6], P(('dom', 'grp')), may hold values from 0 to 31
- owner_map: int32 [128, 72], P(('dom', 'grp')), may hold values from 0 to 127
Outputs:
- coarse_tiles: float32 [64, 1048576], P(None, ('dom', 'grp'))
Inputs may be any that keep to these rules, and one draw needn't show every extreme that they name: `nbr_local`: column 0 is the element itself. A value below 32 is an element of the same device; the value 32 + p * 6 + g stands for the row that neighbour p sends to this device in slot g, and every such ghost value appears on every device. `ap_slot`: each row's 7 * 4 entries name every value from 0 to 7. `tile_slot`: on every device each of the 72 partial tiles is named by some entry.
All inputs are finite; a program needn't handle non-finite values.
Results may differ from a plain program's by a relative error of at most 0.0029.
Values may be sent and summed in bfloat16 or wider, within the bound.
A program may use at most 192 MiB of HBM per device.

v0:
```python
import math

import jax
import jax.numpy as jnp
from jax import lax
from jax.sharding import PartitionSpec as P

KB = 64
KC = 64
NB = 7
PN = 4
QN = 8
OWN = 128


def padded_2(x, sides, width):
    for axis, dim in sides:
        devices, length = (lax.axis_size(axis), x.shape[dim])
        up = [(i, (i + 1) % devices) for i in range(devices)]
        down = [(j, i) for i, j in up]
        last = lax.slice_in_dim(x, length - width, length, axis=dim)
        leading = lax.slice_in_dim(x, 0, width, axis=dim)
        before = lax.ppermute(last, axis, up)
        after = lax.ppermute(leading, axis, down)
        x = jnp.concatenate([before, x, after], axis=dim)
    return x


def local_tiles(a_strips, p_strips, nbr_local, ap_slot, tile_slot, extended, tiles_total):
    rows_here = a_strips.shape[0]
    block_len = math.gcd(rows_here, 32)
    blocks = rows_here // block_len
    tile_ids = jnp.arange(tiles_total, dtype=jnp.int32)

    def regroup(source_array):
        return source_array.reshape((blocks, block_len) + source_array.shape[1:])

    def accumulate(partial_value, inputs):
        a_block, p_block, nbr_block, slot_block, tile_block = inputs
        a_tiles = a_block.reshape(block_len, KB, NB, KB)
        gathered = extended[nbr_block]
        product = jnp.einsum(
            "eijm,ejmn->ejin", a_tiles, gathered, preferred_element_type=jnp.float32
        )
        product = product.reshape(block_len, NB, KB, PN, KC)
        selector = (slot_block[..., None] == jnp.arange(QN, dtype=jnp.int32)).astype(jnp.float32)
        applied = jnp.einsum(
            "ejikc,ejkq->eiqc", product, selector, precision=lax.Precision.HIGHEST
        ).astype(jnp.bfloat16)
        own_tiles = p_block.reshape(block_len, KB, PN, KC)
        contrib = jnp.einsum(
            "emkc,emqd->ekqcd", own_tiles, applied, preferred_element_type=jnp.float32
        )
        placement = (tile_block.reshape(-1)[:, None] == tile_ids[None, :]).astype(jnp.float32)
        added = jnp.einsum(
            "nt,nf->tf", placement, contrib.reshape(-1, KC * KC), precision=lax.Precision.HIGHEST
        )
        return (partial_value + added, None)

    initial = jnp.zeros((tiles_total, KC * KC), jnp.float32)
    inputs = (
        regroup(a_strips),
        regroup(p_strips),
        regroup(nbr_local),
        regroup(ap_slot),
        regroup(tile_slot),
    )
    return lax.scan(accumulate, initial, inputs)[0]


def body(a_strips, p_strips, nbr_local, ap_slot, tile_slot, send_rows, owner_map):
    strip_width = p_strips.shape[2]
    ghost_count = send_rows.shape[2]
    outgoing = p_strips[send_rows.reshape(-1)].reshape(8, ghost_count, KB, strip_width)
    middle = jnp.zeros_like(outgoing[:1])
    cells = jnp.concatenate([outgoing[:4], middle, outgoing[4:]], 0).reshape(
        3, 3, ghost_count, KB, strip_width
    )
    padded = padded_2(cells, (("dom", 0), ("grp", 1)), 1)
    picked = padded[0::2, 0::2].reshape(9, ghost_count, KB, strip_width)
    arrived = jnp.concatenate([picked[:4], picked[5:]], 0)
    extended = jnp.concatenate([p_strips, arrived.reshape(8 * ghost_count, KB, strip_width)], 0)
    tiles_total = owner_map.shape[1]
    slot_count = tiles_total // 9
    partial_value = local_tiles(
        a_strips, p_strips, nbr_local, ap_slot, tile_slot, extended, tiles_total
    )
    parcels = partial_value.reshape(3, 3, slot_count, KC, KC)
    tile_pad = padded_2(parcels, (("dom", 0), ("grp", 1)), 1)
    returned = tile_pad[0::2, 0::2].reshape(tiles_total, KC * KC)
    owner_ids = jnp.arange(OWN, dtype=jnp.int32)
    ownership = (owner_map.reshape(-1)[:, None] == owner_ids[None, :]).astype(jnp.float32)
    owned_tiles = jnp.einsum("tm,tf->mf", ownership, returned, precision=lax.Precision.HIGHEST)
    return owned_tiles.reshape(OWN, KC, KC).transpose(1, 0, 2).reshape(KC, OWN * KC)


def solution(mesh):
    placed = (
        P(("dom", "grp"), None, None),
        P(("dom", "grp"), None, None),
        P(("dom", "grp"), None),
        P(("dom", "grp"), None, None),
        P(("dom", "grp"), None, None),
        P(("dom", "grp"), None, None),
        P(("dom", "grp"), None),
    )
    return jax.shard_map(
        body, mesh=mesh, in_specs=placed, out_specs=P(None, ("dom", "grp")), check_vma=False
    )
```

profile of v0, /device:TPU:7, one launch (start us, length us, event | category | flops | bytes accessed | tf_op | source)
XLA Modules:
  0.0 272.3 jit_solution(17696588424967063886)
XLA Ops:
  0.0 0.7 compare_select_fusion
  0.7 0.1 copy.16
  0.8 0.1 reshape.123
  0.9 0.8 copy.15
  1.6 0.1 reshape.102
  1.7 1.9 gather_fusion
  3.6 0.1 fusion.15
  3.7 1.7 collective-permute-start
  5.4 4.7 %collective-permute-start.1 = (bf16[1,3,6,64,256]{4,3,2,1,0:T(8,128)(2,1)S(1)}, bf16[1,3,6,64,256]{4,3,2,1,0:T(8,128)(2,1)S(1)}, u32[]{:S(2)}, u32[]{:S(2)}) collective-permute-start(bf16[1,3,6,64,256]{4,3,2,1,0:T(8,128)(2,1)S(1)} %bitcast.71), channel_id=1, source_target_pairs={{8,0},{16,8},{24,16},{32,24},{40,32},{48,40},{56,48},{64,56},{72,6... | collective-permute-start | bytes 1769480 | tf_op jit(solution)/shard_map/ppermute | solution.py:24
  10.1 0.1 pad.16.clone
  10.2 0.1 fusion.16
  10.3 0.0 copy-start.1
  10.3 0.2 pad_maximum_fusion.3
  10.5 12.5 %collective-permute-done = bf16[1,3,6,64,256]{4,3,2,1,0:T(8,128)(2,1)S(1)} collective-permute-done((bf16[1,3,6,64,256]{4,3,2,1,0:T(8,128)(2,1)S(1)}, bf16[1,3,6,64,256]{4,3,2,1,0:T(8,128)(2,1)S(1)}, u32[]{:S(2)}, u32[]{:S(2)}) %collective-permute-start) | collective-permute-done | bytes 589856 | tf_op jit(solution)/shard_map/ppermute | solution.py:23
  23.0 0.0 collective-permute-done.1
  23.0 0.8 copy-done.3
  23.9 1.5 pad_maximum_fusion.7
  25.4 1.3 collective-permute-start.2
  26.7 1.8 reshape.108
  28.5 6.4 %reshape.106 = bf16[32,64,7,64]{3,2,1,0:T(8,128)(2,1)} reshape(bf16[32,64,448]{2,1,0:T(8,128)(2,1)} %param.7) | data formatting | bytes 3670016 | tf_op jit(solution)/shard_map/while/body/eval_jaxpr/reshape | solution.py:40
  34.9 0.1 copy.14
  35.0 0.1 copy.13
  35.1 0.1 eq.61
  35.2 0.3 fusion.25
  35.5 2.5 collective-permute-done.2
  38.1 3.7 %collective-permute-done.3 = bf16[5,1,6,64,256]{4,3,2,1,0:T(8,128)(2,1)} collective-permute-done((bf16[5,1,6,64,256]{4,3,2,1,0:T(8,128)(2,1)}, bf16[5,1,6,64,256]{4,3,2,1,0:T(8,128)(2,1)}, u32[]{:S(2)}, u32[]{:S(2)}) %collective-permute-start.3) | collective-permute-done | bytes 983072 | tf_op jit(solution)/shard_map/ppermute | solution.py:24
  41.7 2.7 pad_maximum_fusion.1
  44.4 0.2 slice.76
  44.6 0.0 copy-start.2
  44.6 0.2 fusion.14
  44.8 0.1 pad_maximum_fusion.4
  45.0 0.9 copy-done.2
  45.9 0.2 pad_maximum_fusion.2
  46.1 8.3 %gather_fusion.1 = bf16[224,64,256]{2,1,0:T(8,128)(2,1)} fusion(bf16[80,64,256]{2,1,0:T(8,128)(2,1)S(1)} %pad_maximum_fusion.2, s32[1024]{0:T(1024)S(1)} %get-tuple-element.44), kind=kCustom, calls=%fused_computation.1 | custom fusion | bytes 14680960 | tf_op jit(solution)/shard_map/while/body/eval_jaxpr/gather | solution.py:41
  54.4 11.6 %convolution_bitcast_fusion.1 = f32[32,7,64,256]{3,2,1,0:T(8,128)} fusion(bf16[32,7,64,256]{3,2,1,0:T(8,128)(2,1)} %bitcast.62, bf16[32,64,7,64]{3,2,1,0:T(8,128)(2,1)} %reshape.106), kind=kOutput, calls=%fused_computation.3 | convolution fusion | flops 469762048 | bytes 23855104 | tf_op jit(solution)/shard_map/while/body/eval_jaxpr/eijm,ejmn->ejin/dot_general | solution.py:42
  66.1 25.3 %reshape.107 = f32[32,7,64,4,64]{4,3,2,1,0:T(4,128)} reshape(f32[32,7,64,256]{3,2,1,0:T(8,128)} %convolution_bitcast_fusion.1) | data formatting | bytes 29360128 | tf_op jit(solution)/shard_map/while/body/eval_jaxpr/reshape | solution.py:45
  91.4 26.6 %convolution_bitcast_fusion.2 = bf16[32,8,64,64,1]{3,1,4,2,0:T(8,128)(2,1)} fusion(f32[32,7,64,4,64]{4,3,2,1,0:T(4,128)} %reshape.107, pred[32,7,4,8,1]{3,2,4,1,0:T(4,128)(4,1)S(1)} %fusion.25), kind=kOutput, calls=%fused_computation.9 | convolution fusion | flops 352321536 | bytes 16784384 | tf_op jit(solution)/shard_map/while/body/eval_jaxpr/ejikc,ejkq->eiqc/dot_general | solution.py:47
  118.0 7.0 %copy.24 = bf16[32,8,64,64,1]{2,3,1,0,4:T(8,128)(2,1)} copy(bf16[32,8,64,64,1]{3,1,4,2,0:T(8,128)(2,1)} %convolution_bitcast_fusion.2) | data formatting | bytes 4194304 | tf_op jit(solution)/shard_map/while/body/eval_jaxpr/ejikc,ejkq->eiqc/dot_general | solution.py:47
  124.9 15.3 %convolution_bitcast_fusion = f32[32,4,8,64,64]{3,4,1,2,0:T(8,128)} fusion(bf16[32,8,64,64,1]{2,3,1,0,4:T(8,128)(2,1)} %copy.24, bf16[32,64,4,64,1]{3,2,1,0,4:T(4,128)(2,1)S(1)} %bitcast.63), kind=kOutput, calls=%fused_computation.2 | convolution fusion | flops 536870912 | bytes 19922944 | tf_op jit(solution)/shard_map/while/body/eval_jaxpr/emkc,emqd->ekqcd/dot_general | solution.py:51
  140.2 33.5 %copy.19 = f32[32,4,8,64,64]{4,3,2,1,0:T(8,128)} copy(f32[32,4,8,64,64]{3,4,1,2,0:T(8,128)} %convolution_bitcast_fusion) | data formatting | bytes 33554432 | tf_op jit(solution)/shard_map/while/body/eval_jaxpr/emkc,emqd->ekqcd/transpose | solution.py:51
  173.7 27.9 %reshape.109 = f32[1024,4096]{1,0:T(8,128)} reshape(f32[32,4,8,64,64]{4,3,2,1,0:T(8,128)} %copy.19) | data formatting | bytes 33554432 | tf_op jit(solution)/shard_map/while/body/eval_jaxpr/reshape | solution.py:56
  201.6 10.4 %fusion.4 = f32[72,4096]{1,0:T(8,128)S(1)} fusion(f32[1024,4096]{1,0:T(8,128)} %reshape.109, s32[1024]{0:T(1024)S(1)} %eq.61), kind=kOutput, calls=%fused_computation.19 | convolution fusion | flops 3623952384 | bytes 17960960 | tf_op jit(solution)/shard_map/while/body/eval_jaxpr/nt,nf->tf/dot_general | solution.py:55
  212.0 0.1 fusion.17
  212.1 1.2 slice.80
  213.3 0.0 collective-permute-start.4
  213.3 1.2 slice.82
  214.5 4.9 %collective-permute-start.5 = (f32[1,3,8,64,64]{4,3,2,1,0:T(8,128)}, f32[1,3,8,64,64]{4,3,2,1,0:T(8,128)}, u32[]{:S(2)}, u32[]{:S(2)}) collective-permute-start(f32[1,3,8,64,64]{4,3,2,1,0:T(8,128)} %slice.82), channel_id=1, source_target_pairs={{8,0},{16,8},{24,16},{32,24},{40,32},{48,40},{56,48},{64,56},{72,6... | collective-permute-start | bytes 1179656 | tf_op jit(solution)/shard_map/ppermute | solution.py:24
  219.4 0.9 reshape.110
  220.3 15.0 %collective-permute-done.4 = f32[1,3,8,64,64]{4,3,2,1,0:T(8,128)} collective-permute-done((f32[1,3,8,64,64]{4,3,2,1,0:T(8,128)}, f32[1,3,8,64,64]{4,3,2,1,0:T(8,128)}, u32[]{:S(2)}, u32[]{:S(2)}) %collective-permute-start.4) | collective-permute-done | bytes 393248 | tf_op jit(solution)/shard_map/ppermute | solution.py:23
  235.4 1.2 constant_dynamic-update-slice_fusion.2
  236.6 0.2 constant_dynamic-update-slice_fusion.1
  236.7 1.2 constant_dynamic-update-slice_fusion
  237.9 0.3 fusion.13
  238.3 1.5 collective-permute-start.6
  239.8 14.5 %collective-permute-done.6 = f32[5,1,8,64,64]{4,3,2,1,0:T(8,128)S(1)} collective-permute-done((f32[5,1,8,64,64]{4,3,2,1,0:T(8,128)S(1)}, f32[5,1,8,64,64]{4,3,2,1,0:T(8,128)S(1)}, u32[]{:S(2)}, u32[]{:S(2)}) %collective-permute-start.6) | collective-permute-done | bytes 655392 | tf_op jit(solution)/shard_map/ppermute | solution.py:23
  254.3 3.7 %collective-permute-done.7 = f32[5,1,8,64,64]{4,3,2,1,0:T(8,128)S(1)} collective-permute-done((f32[5,1,8,64,64]{4,3,2,1,0:T(8,128)S(1)}, f32[5,1,8,64,64]{4,3,2,1,0:T(8,128)S(1)}, u32[]{:S(2)}, u32[]{:S(2)}) %collective-permute-start.7) | collective-permute-done | bytes 655392 | tf_op jit(solution)/shard_map/ppermute | solution.py:24
  258.0 1.4 pad_maximum_fusion
  259.5 0.2 slice.85
  259.6 0.0 copy-start.7
  259.6 0.7 reshape.111
  260.4 1.8 copy.20
  262.1 2.7 %convolution_bitcast_fusion.3 = f32[64,128,64]{1,2,0:T(8,128)S(1)} fusion(f32[64,64,72]{2,1,0:T(8,128)} %bitcast.66, s32[72]{0:T(128)S(1)} %bitcast.73), kind=kOutput, calls=%fused_computation.13 | convolution fusion | flops 452994048 | bytes 3277088 | tf_op jit(solution)/shard_map/tm,tf->mf/dot_general | solution.py:93
  264.9 2.7 copy.21
  267.6 4.8 %reshape.112 = f32[64,8192]{1,0:T(8,128)} reshape(f32[64,128,64]{2,1,0:T(8,128)} %copy.21) | data formatting | bytes 4194304 | tf_op jit(solution)/shard_map/reshape | solution.py:94
  (16 shorter events, 0.0 us)
Async XLA Ops:
  3.7 19.3 %collective-permute-start = (bf16[1,3,6,64,256]{4,3,2,1,0:T(8,128)(2,1)S(1)}, bf16[1,3,6,64,256]{4,3,2,1,0:T(8,128)(2,1)S(1)}, u32[]{:S(2)}, u32[]{:S(2)}) collective-permute-start(bf16[1,3,6,64,256]{4,3,2,1,0:T(8,128)(2,1)S(1)} %bitcast.72), channel_id=1, source_target_pairs={{0,8},{8,16},{16,24},{24,32},{32,40},{40,48},{48,56},{56,64},{64,7... | collective-permute-start | bytes 1769480 | tf_op jit(solution)/shard_map/ppermute | solution.py:23
  5.4 17.6 %collective-permute-start.1 = (bf16[1,3,6,64,256]{4,3,2,1,0:T(8,128)(2,1)S(1)}, bf16[1,3,6,64,256]{4,3,2,1,0:T(8,128)(2,1)S(1)}, u32[]{:S(2)}, u32[]{:S(2)}) collective-permute-start(bf16[1,3,6,64,256]{4,3,2,1,0:T(8,128)(2,1)S(1)} %bitcast.71), channel_id=1, source_target_pairs={{8,0},{16,8},{24,16},{32,24},{40,32},{48,40},{56,48},{64,56},{72,6... | collective-permute-start | bytes 1769480 | tf_op jit(solution)/shard_map/ppermute | solution.py:24
  10.3 16.4 %copy-start.1 = (bf16[32,64,256]{2,1,0:T(8,128)(2,1)S(1)}, bf16[32,64,256]{2,1,0:T(8,128)(2,1)}, u32[]{:S(2)}) copy-start(bf16[32,64,256]{2,1,0:T(8,128)(2,1)} %param.8) | copy-start | bytes 3145732
  23.0 0.8 copy-start.3
  25.4 12.7 %collective-permute-start.2 = (bf16[5,1,6,64,256]{4,3,2,1,0:T(8,128)(2,1)}, bf16[5,1,6,64,256]{4,3,2,1,0:T(8,128)(2,1)}, u32[]{:S(2)}, u32[]{:S(2)}) collective-permute-start(bf16[5,1,6,64,256]{4,3,2,1,0:T(8,128)(2,1)} %get-tuple-element.23), channel_id=1, source_target_pairs={{0,1},{1,2},{2,3},{3,4},{4,5},{5,6},{6,7},{7,0},{8,9},{9,10},{10,1... | collective-permute-start | bytes 2949128 | tf_op jit(solution)/shard_map/ppermute | solution.py:23
  26.7 15.0 %collective-permute-start.3 = (bf16[5,1,6,64,256]{4,3,2,1,0:T(8,128)(2,1)}, bf16[5,1,6,64,256]{4,3,2,1,0:T(8,128)(2,1)}, u32[]{:S(2)}, u32[]{:S(2)}) collective-permute-start(bf16[5,1,6,64,256]{4,3,2,1,0:T(8,128)(2,1)} %get-tuple-element.24), channel_id=1, source_target_pairs={{1,0},{2,1},{3,2},{4,3},{5,4},{6,5},{7,6},{0,7},{9,8},{10,9},{11,1... | collective-permute-start | bytes 2949128 | tf_op jit(solution)/shard_map/ppermute | solution.py:24
  28.5 6.4 %copy-start.6 = (s32[32,7,4]{0,2,1:T(4,128)S(1)}, s32[32,7,4]{0,2,1:T(4,128)}, u32[]{:S(2)}) copy-start(s32[32,7,4]{0,2,1:T(4,128)} %param.10) | copy-start | bytes 10756
  28.5 6.5 %copy-start.5 = (s32[32,4,8]{0,2,1:T(8,128)S(1)}, s32[32,4,8]{0,2,1:T(8,128)}, u32[]{:S(2)}) copy-start(s32[32,4,8]{0,2,1:T(8,128)} %param.11) | copy-start | bytes 12292
  28.5 13.2 %copy-start.4 = (bf16[1,3,6,64,256]{4,3,2,1,0:T(8,128)(2,1)S(1)}, bf16[1,3,6,64,256]{4,3,2,1,0:T(8,128)(2,1)}, u32[]{:S(2)}) copy-start(bf16[1,3,6,64,256]{4,3,2,1,0:T(8,128)(2,1)} %copy-done.3) | copy-start | bytes 1769476
  44.6 1.2 copy-start.2
  118.0 7.0 %copy-start = (bf16[32,64,4,64]{3,2,1,0:T(4,128)(2,1)S(1)}, bf16[32,64,4,64]{3,2,1,0:T(4,128)(2,1)}, u32[]{:S(2)}) copy-start(bf16[32,64,4,64]{3,2,1,0:T(4,128)(2,1)} %reshape.108) | copy-start | bytes 3145732
  213.3 22.1 %collective-permute-start.4 = (f32[1,3,8,64,64]{4,3,2,1,0:T(8,128)}, f32[1,3,8,64,64]{4,3,2,1,0:T(8,128)}, u32[]{:S(2)}, u32[]{:S(2)}) collective-permute-start(f32[1,3,8,64,64]{4,3,2,1,0:T(8,128)} %slice.80), channel_id=1, source_target_pairs={{0,8},{8,16},{16,24},{24,32},{32,40},{40,48},{48,56},{56,64},{64,7... | collective-permute-start | bytes 1179656 | tf_op jit(solution)/shard_map/ppermute | solution.py:23
  214.5 22.2 %collective-permute-start.5 = (f32[1,3,8,64,64]{4,3,2,1,0:T(8,128)}, f32[1,3,8,64,64]{4,3,2,1,0:T(8,128)}, u32[]{:S(2)}, u32[]{:S(2)}) collective-permute-start(f32[1,3,8,64,64]{4,3,2,1,0:T(8,128)} %slice.82), channel_id=1, source_target_pairs={{8,0},{16,8},{24,16},{32,24},{40,32},{48,40},{56,48},{64,56},{72,6... | collective-permute-start | bytes 1179656 | tf_op jit(solution)/shard_map/ppermute | solution.py:24
  238.3 16.0 %collective-permute-start.6 = (f32[5,1,8,64,64]{4,3,2,1,0:T(8,128)S(1)}, f32[5,1,8,64,64]{4,3,2,1,0:T(8,128)S(1)}, u32[]{:S(2)}, u32[]{:S(2)}) collective-permute-start(f32[5,1,8,64,64]{4,3,2,1,0:T(8,128)S(1)} %get-tuple-element.21), channel_id=1, source_target_pairs={{0,1},{1,2},{2,3},{3,4},{4,5},{5,6},{6,7},{7,0},{8,9},{9,10},{10,1... | collective-permute-start | bytes 1966088 | tf_op jit(solution)/shard_map/ppermute | solution.py:23
  239.8 18.2 %collective-permute-start.7 = (f32[5,1,8,64,64]{4,3,2,1,0:T(8,128)S(1)}, f32[5,1,8,64,64]{4,3,2,1,0:T(8,128)S(1)}, u32[]{:S(2)}, u32[]{:S(2)}) collective-permute-start(f32[5,1,8,64,64]{4,3,2,1,0:T(8,128)S(1)} %get-tuple-element.22), channel_id=1, source_target_pairs={{1,0},{2,1},{3,2},{4,3},{5,4},{6,5},{7,6},{0,7},{9,8},{10,9},{11,1... | collective-permute-start | bytes 1966088 | tf_op jit(solution)/shard_map/ppermute | solution.py:24
  259.6 2.5 copy-start.7
where the time goes:
time: 274 us; the launch traced here: 272 us
  local copies, waits for them, and re-layouts  132 us (48%)
  matrix products  66.6 us (24%)
  waiting for transfers between devices  52 us (19%)
  starting transfers between devices  14.1 us (5%)
  other arithmetic  7.18 us (3%)
    ppermute x4, waiting for transfers between devices, padded_2(): before = lax.ppermute(last, axis, up)  44.6 us
    transpose x1, local copies, waits for them, and re-layouts, accumulate(): jnp.einsum('emkc,emqd->ekqcd', own_tiles, applied, preferred_element_type...  33.5 us
    reshape x1, local copies, waits for them, and re-layouts, accumulate(): contrib.reshape(-1, KC * KC)  27.9 us
    dot_general x1, matrix products, accumulate(): jnp.einsum('ejikc,ejkq->eiqc', product, selector, precision=lax.Precision...  26.6 us
    reshape x1, local copies, waits for them, and re-layouts, accumulate(): product = product.reshape(block_len, NB, KB, PN, KC)  25.3 us
    dot_general x1, matrix products, accumulate(): jnp.einsum('emkc,emqd->ekqcd', own_tiles, applied, preferred_element_type...  15.3 us
    dot_general x1, matrix products, accumulate(): jnp.einsum('eijm,ejmn->ejin', a_tiles, gathered, preferred_element_type=j...  11.6 us
    dot_general x1, matrix products, accumulate(): jnp.einsum('nt,nf->tf', placement, contrib.reshape(-1, KC * KC), precisio...  10.4 us
  transfers between devices with their start and end apart: 8, of which 6 were waited for; matrix products, arithmetic and copies ran while one was open for 5% of the time, Pallas kernels for 0%

commit v1 on v0

v1 whole, which is shorter than its diff:
```python
import jax
import jax.numpy as jnp
from jax import lax
from jax.experimental import pallas as pl
from jax.experimental.pallas import tpu as pltpu
from jax.sharding import PartitionSpec as P

KB = 64
KC = 64
NB = 7
PN = 4
QN = 8
OWN = 128
MESH = pl.DeviceIdType.MESH
CELLS = [(a, b) for a in (-1, 0, 1) for b in (-1, 0, 1)]
AROUND = [cell for cell in CELLS if cell != (0, 0)]
ORDER = sorted(range(8), key=lambda p: -(abs(AROUND[p][0]) * 2 + abs(AROUND[p][1])))


def device_at(offset):
    rows, cols = lax.axis_size("dom"), lax.axis_size("grp")
    i = lax.rem(lax.axis_index("dom") + offset[0] + rows, rows)
    j = lax.rem(lax.axis_index("grp") + offset[1] + cols, cols)
    return (i, j)


def greet():
    barrier = pltpu.get_barrier_semaphore()
    for offset in AROUND:
        pl.semaphore_signal(barrier, inc=1, device_id=device_at(offset), device_id_type=MESH)
    return barrier


def ghost_kernel(send_rows, p_ref, ghost_ref, outbox, send_sem, recv_sem):
    slots = send_rows.shape[0]
    barrier = greet()
    for p in ORDER:
        for g in range(slots):
            outbox[p * slots + g] = p_ref[send_rows[g, 0, p]]
    pl.semaphore_wait(barrier, 8)
    copies = []
    for p in ORDER:
        copies.append(
            pltpu.make_async_remote_copy(
                src_ref=outbox.at[pl.ds(p * slots, slots)],
                dst_ref=ghost_ref.at[pl.ds((7 - p) * slots, slots)],
                send_sem=send_sem.at[p],
                recv_sem=recv_sem.at[7 - p],
                device_id=device_at(AROUND[p]),
                device_id_type=MESH,
            )
        )
        copies[-1].start()
    for copy in copies:
        copy.wait()


def local_kernel(
    nbr, ap, ts, a_ref, p_hbm, g_hbm, out_ref, ext, acc_a, acc_b, part_a, part_b, part_c, part_d, sem
):
    n = a_ref.shape[0]
    own = pltpu.make_async_copy(p_hbm, ext.at[pl.ds(0, n)], sem.at[0])
    ghosts = pltpu.make_async_copy(g_hbm, ext.at[pl.ds(n, g_hbm.shape[0])], sem.at[1])
    own.start()
    ghosts.start()
    parts = (part_a, part_b, part_c, part_d)
    for part in parts:
        part[...] = jnp.zeros_like(part)
    own.wait()
    ghosts.wait()
    low = lax.broadcasted_iota(jnp.int32, (KB, 128), 1) < KC

    def element(e, carry):
        acc_a[...] = jnp.zeros_like(acc_a)
        acc_b[...] = jnp.zeros_like(acc_b)
        for j in range(NB):
            x = ext[nbr[j, e]]
            prod = jnp.dot(a_ref[e, :, j * KB : (j + 1) * KB], x, preferred_element_type=jnp.float32)
            for half in range(2):
                chunk = prod[:, half * 128 : (half + 1) * 128]
                acc_a[ap[j, 2 * half, e]] += chunk
                acc_b[ap[j, 2 * half + 1, e]] += chunk
        columns = []
        for u in range(QN // 2):
            even = jnp.where(low, acc_a[2 * u], acc_b[2 * u])
            odd = jnp.where(low, acc_a[2 * u + 1], acc_b[2 * u + 1])
            even = even + pltpu.roll(even, KC, 1)
            odd = odd + pltpu.roll(odd, KC, 1)
            columns.append(jnp.where(low, even, odd).astype(jnp.bfloat16))
        applied = jnp.concatenate(columns, axis=1)
        contrib = lax.dot_general(
            ext[e], applied, (((0,), (0,)), ((), ())), preferred_element_type=jnp.float32
        )
        for k in range(PN):
            first, second = parts[:2] if k % 2 == 0 else parts[2:]
            for u in range(QN // 2):
                chunk = contrib[k * KC : (k + 1) * KC, u * 128 : (u + 1) * 128]
                first[ts[k, 2 * u, e]] += chunk
                second[ts[k, 2 * u + 1, e]] += chunk
        return carry

    lax.fori_loop(0, n, element, 0)

    def tile(t):
        total = jnp.where(low, part_a[t] + part_c[t], part_b[t] + part_d[t])
        return total + pltpu.roll(total, KC, 1)

    def pack(i, carry):
        out_ref[i] = jnp.where(low, tile(2 * i), tile(2 * i + 1)).astype(jnp.bfloat16)
        return carry

    lax.fori_loop(0, out_ref.shape[0], pack, 0)


def parcel_kernel(tiles_ref, returned_ref, send_sem, recv_sem, own_sem):
    pairs = tiles_ref.shape[0] // 9
    barrier = greet()
    own = pltpu.make_async_copy(
        tiles_ref.at[pl.ds(4 * pairs, pairs)], returned_ref.at[pl.ds(4 * pairs, pairs)], own_sem
    )
    own.start()
    pl.semaphore_wait(barrier, 8)
    copies = []
    for p in ORDER:
        cell = CELLS.index(AROUND[p])
        copies.append(
            pltpu.make_async_remote_copy(
                src_ref=tiles_ref.at[pl.ds(cell * pairs, pairs)],
                dst_ref=returned_ref.at[pl.ds((8 - cell) * pairs, pairs)],
                send_sem=send_sem.at[p],
                recv_sem=recv_sem.at[7 - p],
                device_id=device_at(AROUND[p]),
                device_id_type=MESH,
            )
        )
        copies[-1].start()
    own.wait()
    for copy in copies:
        copy.wait()


def owner_kernel(owner_map, returned_ref, out_ref):
    out_ref[...] = jnp.zeros_like(out_ref)
    low = lax.broadcasted_iota(jnp.int32, (KC, 128), 1) < KC

    def add(i, carry):
        pair = returned_ref[i].astype(jnp.float32)
        turned = pltpu.roll(pair, KC, 1)
        for side, same, other in ((0, pair, turned), (1, turned, pair)):
            m = owner_map[0, 2 * i + side]
            at = pl.ds(pl.multiple_of((m // 2) * 128, 128), 128)
            even = lax.rem(m, 2) == 0
            keep = jnp.logical_xor(low, jnp.logical_not(even))
            value = jnp.where(low, same, other)
            out_ref[:, at] += jnp.where(keep, value, 0.0)
        return carry

    lax.fori_loop(0, returned_ref.shape[0], add, 0)


def body(a_strips, p_strips, nbr_local, ap_slot, tile_slot, send_rows, owner_map):
    width = p_strips.shape[2]
    slots = send_rows.shape[2]
    smem = pl.BlockSpec(memory_space=pltpu.SMEM)
    vmem = pl.BlockSpec(memory_space=pltpu.VMEM)
    anywhere = pl.BlockSpec(memory_space=pl.ANY)
    tiles_total = owner_map.shape[1]
    n = a_strips.shape[0]
    ghosts = pl.pallas_call(
        ghost_kernel,
        out_shape=jax.ShapeDtypeStruct((8 * slots, KB, width), jnp.bfloat16),
        in_specs=[smem, vmem],
        out_specs=anywhere,
        scratch_shapes=[
            pltpu.VMEM((8 * slots, KB, width), jnp.bfloat16),
            pltpu.SemaphoreType.DMA((8,)),
            pltpu.SemaphoreType.DMA((8,)),
        ],
        compiler_params=pltpu.CompilerParams(collective_id=0, has_side_effects=True),
    )(send_rows.transpose(2, 0, 1), p_strips)
    tiles = pl.pallas_call(
        local_kernel,
        out_shape=jax.ShapeDtypeStruct((tiles_total // 2, KC, 2 * KC), jnp.bfloat16),
        in_specs=[smem, smem, smem, vmem, anywhere, anywhere],
        out_specs=vmem,
        scratch_shapes=[
            pltpu.VMEM((n + 8 * slots, KB, width), jnp.bfloat16),
            pltpu.VMEM((QN, KB, 2 * KC), jnp.float32),
            pltpu.VMEM((QN, KB, 2 * KC), jnp.float32),
        ]
        + [pltpu.VMEM((tiles_total, KC, 2 * KC), jnp.float32)] * 4
        + [pltpu.SemaphoreType.DMA((2,))],
    )(
        nbr_local.transpose(1, 0),
        ap_slot.transpose(1, 2, 0),
        tile_slot.transpose(1, 2, 0),
        a_strips,
        p_strips,
        ghosts,
    )
    returned = pl.pallas_call(
        parcel_kernel,
        out_shape=jax.ShapeDtypeStruct(tiles.shape, tiles.dtype),
        in_specs=[vmem],
        out_specs=vmem,
        scratch_shapes=[
            pltpu.SemaphoreType.DMA((8,)),
            pltpu.SemaphoreType.DMA((8,)),
            pltpu.SemaphoreType.DMA,
        ],
        compiler_params=pltpu.CompilerParams(collective_id=1, has_side_effects=True),
    )(tiles)
    return pl.pallas_call(
        owner_kernel,
        out_shape=jax.ShapeDtypeStruct((KC, OWN * KC), jnp.float32),
        in_specs=[smem, vmem],
        out_specs=vmem,
    )(owner_map, returned)


def solution(mesh):
    placed = (
        P(("dom", "grp"), None, None),
        P(("dom", "grp"), None, None),
        P(("dom", "grp"), None),
        P(("dom", "grp"), None, None),
        P(("dom", "grp"), None, None),
        P(("dom", "grp"), None, None),
        P(("dom", "grp"), None),
    )
    return jax.shard_map(
        body, mesh=mesh, in_specs=placed, out_specs=P(None, ("dom", "grp")), check_vma=False
    )
```

time: 274 us -> 70.4 us (0.26)
  local copies, waits for them, and re-layouts: 132 us -> 0 us
  Pallas kernels: 0 us -> 69.7 us
  matrix products: 66.6 us -> 0 us
  waiting for transfers between devices: 52 us -> 0 us
  starting transfers between devices: 14.1 us -> 0 us
  other arithmetic: 7.18 us -> 0 us
    pallas_call x0 -> x4, Pallas kernels: none -> 69.7 us  [the longest x1 28.4 us: body(): pl.pallas_call(local_kernel, out_shape=jax.ShapeDtypeStruct((tiles_total...]
    reshape x9 -> x0, local copies, waits for them, and re-layouts: 69.6 us -> none  [the longest x1 27.9 us: accumulate(): contrib.reshape(-1, KC * KC)]
    dot_general x5 -> x0, matrix products: 66.6 us -> none  [the longest x1 26.6 us: accumulate(): jnp.einsum('ejikc,ejkq->eiqc', product, selector, precision=lax.Precision...]
    ppermute x8 -> x0, waiting for transfers between devices: 52 us -> none  [the longest x4 44.6 us: padded_2(): before = lax.ppermute(last, axis, up)]
    transpose x2 -> x0, local copies, waits for them, and re-layouts: 36.2 us -> none  [the longest x1 33.5 us: accumulate(): jnp.einsum('emkc,emqd->ekqcd', own_tiles, applied, preferred_element_type...]
    ppermute x8 -> x0, starting transfers between devices: 14.1 us -> none  [the longest x4 9.53 us: padded_2(): after = lax.ppermute(leading, axis, down)]
    gather x2 -> x0, local copies, waits for them, and re-layouts: 10.2 us -> none  [the longest x1 8.34 us: accumulate(): gathered = extended[nbr_block]]
    dot_general x1 -> x0, local copies, waits for them, and re-layouts: 6.95 us -> none  [accumulate(): jnp.einsum('ejikc,ejkq->eiqc', product, selector, precision=lax.Precision...]
  transfers between devices with their start and end apart: 8 -> 0, of which waited for: 6 -> 0; matrix products, arithmetic and copies ran while one was open for 5% -> 0% of each run, Pallas kernels for 0% -> 0%
where the time goes in v1:
time: 70.4 us; the launch traced here: 69.7 us
  Pallas kernels  69.7 us (99%)
    pallas_call x1, Pallas kernels, body(): pl.pallas_call(local_kernel, out_shape=jax.ShapeDtypeStruct((tiles_total...  28.4 us
    pallas_call x1, Pallas kernels, body(): pl.pallas_call(ghost_kernel, out_shape=jax.ShapeDtypeStruct((8 * slots, K...  21.9 us
    pallas_call x1, Pallas kernels, body(): pl.pallas_call(parcel_kernel, out_shape=jax.ShapeDtypeStruct(tiles.shape,...  13.9 us
    pallas_call x1, Pallas kernels, body(): pl.pallas_call(owner_kernel, out_shape=jax.ShapeDtypeStruct((KC, OWN * KC...  5.54 us

profile of v1, /device:TPU:7, one launch (start us, length us, event | category | flops | bytes accessed | tf_op | source)
XLA Modules:
  0.0 69.7 jit_solution(8300916995157577574)
XLA Ops:
  0.0 21.9 %shard_map.73.g_hbm = bf16[48,64,256]{2,1,0:T(8,128)(2,1)} custom-call(s32[6,1,8]{2,1,0:T(1,128)} %bitcast.7, bf16[32,64,256]{2,1,0:T(8,128)(2,1)} %p_hbm.1), custom_call_target="tpu_custom_call" | custom-call | tf_op jit(solution)/shard_map/pallas_call | solution.py:169
  21.9 28.4 %shard_map.74.tiles_ref = bf16[36,64,128]{2,1,0:T(8,128)(2,1)} custom-call(s32[7,32]{1,0:T(8,128)} %bitcast.6, s32[7,4,32]{2,1,0:T(4,128)} %bitcast.5, s32[4,8,32]{2,1,0:T(8,128)} %bitcast.4, bf16[32,64,448]{2,1,0:T(8,128)(2,1)} %a_ref.1, bf16[32,64,256]{2,1,0:T(8,128)(2,1)} %p_hbm.1, bf16[48,64,256]{2,1,0:T(8,128)(2,1)} %shard_map.73.g_hbm), custom_call_target="tpu_custom_call" | custom-call | tf_op jit(solution)/shard_map/pallas_call | solution.py:181
  50.3 13.9 %shard_map.75.returned_ref = bf16[36,64,128]{2,1,0:T(8,128)(2,1)} custom-call(bf16[36,64,128]{2,1,0:T(8,128)(2,1)} %shard_map.74.tiles_ref), custom_call_target="tpu_custom_call" | custom-call | tf_op jit(solution)/shard_map/pallas_call | solution.py:201
  64.2 5.5 %shard_map.76 = f32[64,8192]{1,0:T(8,128)} custom-call(s32[1,72]{1,0:T(1,128)} %owner_map.1, bf16[36,64,128]{2,1,0:T(8,128)(2,1)} %shard_map.75.returned_ref), custom_call_target="tpu_custom_call" | custom-call | tf_op jit(solution)/shard_map/pallas_call | solution.py:213

commit v2 on v1

v2 whole, which is shorter than its diff:
```python
import jax
import jax.numpy as jnp
from jax import lax
from jax.experimental import pallas as pl
from jax.experimental.pallas import tpu as pltpu
from jax.sharding import PartitionSpec as P

KB = 64
KC = 64
NB = 7
PN = 4
QN = 8
OWN = 128
GROUP = 4
MESH = pl.DeviceIdType.MESH
CELLS = [(a, b) for a in (-1, 0, 1) for b in (-1, 0, 1)]
AROUND = [cell for cell in CELLS if cell != (0, 0)]
ORDER = sorted(range(8), key=lambda p: -(abs(AROUND[p][0]) * 2 + abs(AROUND[p][1])))


def device_at(offset):
    rows, cols = lax.axis_size("dom"), lax.axis_size("grp")
    i = lax.rem(lax.axis_index("dom") + offset[0] + rows, rows)
    j = lax.rem(lax.axis_index("grp") + offset[1] + cols, cols)
    return (i, j)


def greet():
    barrier = pltpu.get_barrier_semaphore()
    for offset in AROUND:
        pl.semaphore_signal(barrier, inc=1, device_id=device_at(offset), device_id_type=MESH)
    return barrier


def folded(x):
    turned = x.T
    half = KC // 2
    blocks = [
        jnp.concatenate(
            [turned[k * KC : k * KC + half], turned[k * KC + half : (k + 1) * KC]], axis=1
        )
        for k in range(PN)
    ]
    return jnp.concatenate(blocks, axis=0)


def ghost_kernel(
    send_rows, p_ref, ext_ref, outbox, inbox, own_rows, ghost_rows, send_sem, recv_sem, out_sem
):
    slots = send_rows.shape[0]
    n = p_ref.shape[0]
    barrier = greet()
    for p in ORDER:
        for g in range(slots):
            outbox[p * slots + g] = p_ref[send_rows[g, 0, p]]
    pl.semaphore_wait(barrier, 8)
    copies = {}
    for p in ORDER:
        copies[p] = pltpu.make_async_remote_copy(
            src_ref=outbox.at[pl.ds(p * slots, slots)],
            dst_ref=inbox.at[pl.ds((7 - p) * slots, slots)],
            send_sem=send_sem.at[p],
            recv_sem=recv_sem.at[7 - p],
            device_id=device_at(AROUND[p]),
            device_id_type=MESH,
        )
        copies[p].start()

    def fold_own(r, carry):
        own_rows[r] = folded(p_ref[r])
        return carry

    lax.fori_loop(0, n, fold_own, 0)
    written = [pltpu.make_async_copy(own_rows, ext_ref.at[pl.ds(0, n)], out_sem.at[8])]
    written[0].start()
    for p in reversed(ORDER):
        copies[p].wait_recv()
        first = (7 - p) * slots
        for g in range(slots):
            ghost_rows[first + g] = folded(inbox[first + g])
        written.append(
            pltpu.make_async_copy(
                ghost_rows.at[pl.ds(first, slots)],
                ext_ref.at[pl.ds(n + first, slots)],
                out_sem.at[7 - p],
            )
        )
        written[-1].start()
    for p in ORDER:
        copies[p].wait_send()
    for copy in written:
        copy.wait()


def doubled(chunk, low):
    zero = jnp.zeros_like(chunk)
    left = jnp.where(low, chunk, zero)
    right = jnp.where(low, zero, chunk)
    return left, pltpu.roll(left, KB, 1), pltpu.roll(right, KB, 1), right


def local_kernel(nbr, ap, ts, a_ref, p_ref, x_ref, out_ref, *scratch):
    n = a_ref.shape[0]
    half = KC // 2
    accs = [scratch[2 * u : 2 * u + 2] for u in range(GROUP)]
    part_a, part_b, part_c, part_d = scratch[2 * GROUP :]
    parts = ((part_a, part_b), (part_c, part_d))
    for part in scratch[2 * GROUP :]:
        part[...] = jnp.zeros_like(part)
    low = lax.broadcasted_iota(jnp.int32, (KB, 2 * KB), 1) < KB
    zeros = jnp.zeros((KB, 2 * KB), jnp.bfloat16)

    def apply(e, acc):
        for one in acc:
            one[...] = jnp.zeros_like(one)
        for first in range(0, NB, 2):
            members = [j for j in (first, first + 1) if j < NB]
            if len(members) == 2:
                xx, x1, y0, yy = doubled(a_ref[e, :, first * KB : (first + 2) * KB], low)
                rows = ((xx, zeros), (x1, zeros), (zeros, y0), (zeros, yy))
                weights = jnp.concatenate([jnp.concatenate(row, axis=1) for row in rows], axis=0)
                source = jnp.concatenate([x_ref[nbr[j, e]] for j in members], axis=1)
            else:
                only = jnp.concatenate([a_ref[e, :, first * KB :], zeros[:, :KB]], axis=1)
                weights = jnp.concatenate([only, pltpu.roll(only, KB, 1)], axis=0)
                source = x_ref[nbr[first, e]]
            product = lax.dot_general(
                source, weights, (((1,), (1,)), ((), ())), preferred_element_type=jnp.float32
            )
            for s, j in enumerate(members):
                for k in range(PN):
                    acc[k % 2][ap[j, k, e]] += product[
                        k * half : (k + 1) * half, s * 2 * KB : (s + 1) * 2 * KB
                    ]
        return (acc[0][...] + acc[1][...]).astype(jnp.bfloat16).reshape(QN * half, 2 * KB)

    def project(e, applied):
        xx0, x10, y00, yy0 = doubled(p_ref[e, :, : 2 * KC], low)
        xx1, x11, y01, yy1 = doubled(p_ref[e, :, 2 * KC :], low)
        weights = jnp.concatenate(
            [
                jnp.concatenate([xx0, y00, xx1, y01], axis=1),
                jnp.concatenate([x10, yy0, x11, yy1], axis=1),
            ],
            axis=0,
        )
        contrib = jnp.dot(applied, weights, preferred_element_type=jnp.float32)
        for q in range(QN):
            for k in range(PN):
                parts[k % 2][q % 2][ts[k, q, e]] += contrib[
                    q * half : (q + 1) * half, k * 2 * KC : (k + 1) * 2 * KC
                ]

    def group(i, carry):
        applied = [apply(i * GROUP + u, accs[u]) for u in range(GROUP)]
        for u in range(GROUP):
            project(i * GROUP + u, applied[u])
        return carry

    lax.fori_loop(0, n // GROUP, group, 0)

    def pack(t, carry):
        out_ref[t] = (part_a[t] + part_b[t] + part_c[t] + part_d[t]).astype(jnp.bfloat16)
        return carry

    lax.fori_loop(0, out_ref.shape[0], pack, 0, unroll=8)


def unfolded(first, second):
    rows = [t[:, h * KC : (h + 1) * KC] for t in (first, second) for h in range(2)]
    return jnp.concatenate(rows, axis=0).T


def parcel_kernel(tiles_ref, returned_ref, inbox, send_sem, recv_sem):
    slots = tiles_ref.shape[0] // 9
    barrier = greet()
    pl.semaphore_wait(barrier, 8)
    copies = {}
    for p in ORDER:
        cell = CELLS.index(AROUND[p])
        copies[p] = pltpu.make_async_remote_copy(
            src_ref=tiles_ref.at[pl.ds(cell * slots, slots)],
            dst_ref=inbox.at[pl.ds((8 - cell) * slots, slots)],
            send_sem=send_sem.at[p],
            recv_sem=recv_sem.at[7 - p],
            device_id=device_at(AROUND[p]),
            device_id_type=MESH,
        )
        copies[p].start()

    def settle(source, cell):
        for t in range(cell * slots, (cell + 1) * slots, 2):
            returned_ref[t // 2] = unfolded(source[t], source[t + 1])

    settle(tiles_ref, 4)
    for p in reversed(ORDER):
        copies[p].wait_recv()
        settle(inbox, 8 - CELLS.index(AROUND[p]))
    for p in ORDER:
        copies[p].wait_send()


def owner_kernel(owner_map, returned_ref, out_ref):
    out_ref[...] = jnp.zeros_like(out_ref)
    low = lax.broadcasted_iota(jnp.int32, (KC, 128), 1) < KC

    def add(i, carry):
        pair = returned_ref[i].astype(jnp.float32)
        turned = pltpu.roll(pair, KC, 1)
        for side, same, other in ((0, pair, turned), (1, turned, pair)):
            m = owner_map[0, 2 * i + side]
            at = pl.ds(pl.multiple_of((m // 2) * 128, 128), 128)
            even = lax.rem(m, 2) == 0
            keep = jnp.logical_xor(low, jnp.logical_not(even))
            value = jnp.where(low, same, other)
            out_ref[:, at] += jnp.where(keep, value, 0.0)
        return carry

    lax.fori_loop(0, returned_ref.shape[0], add, 0)


def body(a_strips, p_strips, nbr_local, ap_slot, tile_slot, send_rows, owner_map):
    width = p_strips.shape[2]
    slots = send_rows.shape[2]
    smem = pl.BlockSpec(memory_space=pltpu.SMEM)
    vmem = pl.BlockSpec(memory_space=pltpu.VMEM)
    anywhere = pl.BlockSpec(memory_space=pl.ANY)
    tiles_total = owner_map.shape[1]
    n = a_strips.shape[0]
    folded_rows = pltpu.VMEM((8 * slots, 2 * KC, 2 * KB), jnp.bfloat16)
    raw_rows = pltpu.VMEM((8 * slots, KB, width), jnp.bfloat16)
    extended = pl.pallas_call(
        ghost_kernel,
        out_shape=jax.ShapeDtypeStruct((n + 8 * slots, 2 * KC, 2 * KB), jnp.bfloat16),
        in_specs=[smem, vmem],
        out_specs=anywhere,
        scratch_shapes=[
            raw_rows,
            raw_rows,
            pltpu.VMEM((n, 2 * KC, 2 * KB), jnp.bfloat16),
            folded_rows,
            pltpu.SemaphoreType.DMA((8,)),
            pltpu.SemaphoreType.DMA((8,)),
            pltpu.SemaphoreType.DMA((9,)),
        ],
        compiler_params=pltpu.CompilerParams(collective_id=0, has_side_effects=True),
    )(send_rows.transpose(2, 0, 1), p_strips)
    tiles = pl.pallas_call(
        local_kernel,
        out_shape=jax.ShapeDtypeStruct((tiles_total, KC // 2, 2 * KC), jnp.bfloat16),
        in_specs=[smem, smem, smem, vmem, vmem, vmem],
        out_specs=vmem,
        scratch_shapes=[pltpu.VMEM((QN, KC // 2, 2 * KB), jnp.float32)] * (2 * GROUP)
        + [pltpu.VMEM((tiles_total, KC // 2, 2 * KC), jnp.float32)] * 4,
    )(
        nbr_local.transpose(1, 0),
        ap_slot.transpose(1, 2, 0),
        tile_slot.transpose(1, 2, 0),
        a_strips,
        p_strips,
        extended,
    )
    returned = pl.pallas_call(
        parcel_kernel,
        out_shape=jax.ShapeDtypeStruct((tiles_total // 2, KC, 2 * KC), jnp.bfloat16),
        in_specs=[vmem],
        out_specs=vmem,
        scratch_shapes=[
            pltpu.VMEM(tiles.shape, tiles.dtype),
            pltpu.SemaphoreType.DMA((8,)),
            pltpu.SemaphoreType.DMA((8,)),
        ],
        compiler_params=pltpu.CompilerParams(collective_id=1, has_side_effects=True),
    )(tiles)
    return pl.pallas_call(
        owner_kernel,
        out_shape=jax.ShapeDtypeStruct((KC, OWN * KC), jnp.float32),
        in_specs=[smem, vmem],
        out_specs=vmem,
    )(owner_map, returned)


def solution(mesh):
    placed = (
        P(("dom", "grp"), None, None),
        P(("dom", "grp"), None, None),
        P(("dom", "grp"), None),
        P(("dom", "grp"), None, None),
        P(("dom", "grp"), None, None),
        P(("dom", "grp"), None, None),
        P(("dom", "grp"), None),
    )
    return jax.shard_map(
        body, mesh=mesh, in_specs=placed, out_specs=P(None, ("dom", "grp")), check_vma=False
    )
```

time: 70.4 us -> 57.1 us (0.81)
  Pallas kernels: 69.7 us -> 56.9 us
    pallas_call x3, Pallas kernels: 64.2 us -> 51.4 us  [the longest x1 23.9 us: body(): pl.pallas_call(ghost_kernel, out_shape=jax.ShapeDtypeStruct((n + 8 * slot...]
where the time goes in v2:
time: 57.1 us; the launch traced here: 56.9 us
  Pallas kernels  56.9 us (100%)
    pallas_call x1, Pallas kernels, body(): pl.pallas_call(ghost_kernel, out_shape=jax.ShapeDtypeStruct((n + 8 * slot...  23.9 us
    pallas_call x1, Pallas kernels, body(): pl.pallas_call(parcel_kernel, out_shape=jax.ShapeDtypeStruct((tiles_total...  15 us
    pallas_call x1, Pallas kernels, body(): pl.pallas_call(local_kernel, out_shape=jax.ShapeDtypeStruct((tiles_total,...  12.5 us
    pallas_call x1, Pallas kernels, body(): pl.pallas_call(owner_kernel, out_shape=jax.ShapeDtypeStruct((KC, OWN * KC...  5.54 us

profile of v2, /device:TPU:7, one launch (start us, length us, event | category | flops | bytes accessed | tf_op | source)
XLA Modules:
  0.0 56.9 jit_solution(11601328486128682326)
XLA Ops:
  0.0 23.9 %shard_map.73.x_ref = bf16[80,128,128]{2,1,0:T(8,128)(2,1)} custom-call(s32[6,1,8]{2,1,0:T(1,128)} %bitcast.7, bf16[32,64,256]{2,1,0:T(8,128)(2,1)} %p_ref.3), custom_call_target="tpu_custom_call" | custom-call | tf_op jit(solution)/shard_map/pallas_call | solution.py:232
  23.9 12.5 %shard_map.74.tiles_ref = bf16[72,32,128]{2,1,0:T(8,128)(2,1)} custom-call(s32[7,32]{1,0:T(8,128)} %bitcast.6, s32[7,4,32]{2,1,0:T(4,128)} %bitcast.5, s32[4,8,32]{2,1,0:T(8,128)} %bitcast.4, bf16[32,64,448]{2,1,0:T(8,128)(2,1)} %a_ref.1, bf16[32,64,256]{2,1,0:T(8,128)(2,1)} %p_ref.3, bf16[80,128,128]{2,1,0:T(8,128)(2,1)} %shard_map.73.x_ref), custom_call_target="tpu_custom_call" | custom-call | tf_op jit(solution)/shard_map/pallas_call | solution.py:248
  36.4 15.0 %shard_map.75.returned_ref = bf16[36,64,128]{2,1,0:T(8,128)(2,1)} custom-call(bf16[72,32,128]{2,1,0:T(8,128)(2,1)} %shard_map.74.tiles_ref), custom_call_target="tpu_custom_call" | custom-call | tf_op jit(solution)/shard_map/pallas_call | solution.py:263
  51.4 5.5 %shard_map.76 = f32[64,8192]{1,0:T(8,128)} custom-call(s32[1,72]{1,0:T(1,128)} %owner_map.1, bf16[36,64,128]{2,1,0:T(8,128)(2,1)} %shard_map.75.returned_ref), custom_call_target="tpu_custom_call" | custom-call | tf_op jit(solution)/shard_map/pallas_call | solution.py:275

commit v3 on v2

--- a/solution.py
+++ b/solution.py
@@ -11,7 +11,7 @@
 PN = 4
 QN = 8
 OWN = 128
-GROUP = 4
+GROUP = 8
 MESH = pl.DeviceIdType.MESH
 CELLS = [(a, b) for a in (-1, 0, 1) for b in (-1, 0, 1)]
 AROUND = [cell for cell in CELLS if cell != (0, 0)]
@@ -243,7 +243,7 @@
             pltpu.SemaphoreType.DMA((8,)),
             pltpu.SemaphoreType.DMA((9,)),
         ],
-        compiler_params=pltpu.CompilerParams(collective_id=0, has_side_effects=True),
+        compiler_params=pltpu.CompilerParams(collective_id=0, has_side_effects=True, vmem_limit_bytes=12 << 20),
     )(send_rows.transpose(2, 0, 1), p_strips)
     tiles = pl.pallas_call(
         local_kernel,
@@ -252,6 +252,7 @@
         out_specs=vmem,
         scratch_shapes=[pltpu.VMEM((QN, KC // 2, 2 * KB), jnp.float32)] * (2 * GROUP)
         + [pltpu.VMEM((tiles_total, KC // 2, 2 * KC), jnp.float32)] * 4,
+        compiler_params=pltpu.CompilerParams(vmem_limit_bytes=20 << 20),
     )(
         nbr_local.transpose(1, 0),
         ap_slot.transpose(1, 2, 0),
@@ -270,13 +271,14 @@
             pltpu.SemaphoreType.DMA((8,)),
             pltpu.SemaphoreType.DMA((8,)),
         ],
-        compiler_params=pltpu.CompilerParams(collective_id=1, has_side_effects=True),
+        compiler_params=pltpu.CompilerParams(collective_id=1, has_side_effects=True, vmem_limit_bytes=8 << 20),
     )(tiles)
     return pl.pallas_call(
         owner_kernel,
         out_shape=jax.ShapeDtypeStruct((KC, OWN * KC), jnp.float32),
         in_specs=[smem, vmem],
         out_specs=vmem,
+        compiler_params=pltpu.CompilerParams(vmem_limit_bytes=8 << 20),
     )(owner_map, returned)
 
 

time: 57.1 us -> 53.7 us (0.940)
  Pallas kernels: 56.9 us -> 51.5 us
  local copies, waits for them, and re-layouts: 0 us -> 1.95 us
    pallas_call x1, Pallas kernels: 12.5 us -> 9.25 us  [body(): pl.pallas_call(local_kernel, out_shape=jax.ShapeDtypeStruct((tiles_total,...]
    unnamed x0 -> x16, local copies, waits for them, and re-layouts: none -> 1.95 us
    pallas_call x1, Pallas kernels: 15 us -> 13.1 us  [body(): pl.pallas_call(parcel_kernel, out_shape=jax.ShapeDtypeStruct((tiles_total...]
where the time goes in v3:
time: 53.7 us; the launch traced here: 53.6 us
  Pallas kernels  51.5 us (96%)
  local copies, waits for them, and re-layouts  1.95 us (4%)
    pallas_call x1, Pallas kernels, body(): pl.pallas_call(ghost_kernel, out_shape=jax.ShapeDtypeStruct((n + 8 * slot...  24.1 us
    pallas_call x1, Pallas kernels, body(): pl.pallas_call(parcel_kernel, out_shape=jax.ShapeDtypeStruct((tiles_total...  13.1 us
    pallas_call x1, Pallas kernels, body(): pl.pallas_call(local_kernel, out_shape=jax.ShapeDtypeStruct((tiles_total,...  9.25 us
    pallas_call x1, Pallas kernels, body(): pl.pallas_call(owner_kernel, out_shape=jax.ShapeDtypeStruct((KC, OWN * KC...  5.01 us
    unnamed x16, local copies, waits for them, and re-layouts  1.95 us

profile of v3, /device:TPU:7, one launch (start us, length us, event | category | flops | bytes accessed | tf_op | source)
XLA Modules:
  0.0 53.6 jit_solution(5389244693244115220)
XLA Ops:
  0.0 0.0 copy-start.5
  0.0 0.0 copy-start
  0.0 1.2 %copy-done = bf16[32,64,256]{2,1,0:T(8,128)(2,1)S(1)} copy-done((bf16[32,64,256]{2,1,0:T(8,128)(2,1)S(1)}, bf16[32,64,256]{2,1,0:T(8,128)(2,1)}, u32[]{:S(2)}) %copy-start) | copy-done | bytes 1048600
  1.2 0.0 copy-start.6
  1.2 0.7 %copy-done.6 = s32[1,8,6]{1,0,2:T(1,128)S(1)} copy-done((s32[1,8,6]{1,0,2:T(1,128)S(1)}, s32[1,8,6]{1,0,2:T(1,128)}, u32[]{:S(2)}) %copy-start.6) | copy-done | bytes 216
  1.9 0.0 copy-start.1
  1.9 0.0 copy-start.2
  1.9 0.0 copy-start.3
  1.9 0.0 copy-start.4
  1.9 24.1 %shard_map.73.x_ref = bf16[80,128,128]{2,1,0:T(8,128)(2,1)S(1)} custom-call(s32[6,1,8]{2,1,0:T(1,128)S(1)} %bitcast.7, bf16[32,64,256]{2,1,0:T(8,128)(2,1)S(1)} %copy-done), custom_call_target="tpu_custom_call" | custom-call | tf_op jit(solution)/shard_map/pallas_call | solution.py:232
  26.1 0.0 copy-done.5
  26.1 0.0 copy-done.1
  26.1 0.0 copy-done.2
  26.1 0.0 copy-done.3
  26.1 0.0 copy-done.4
  26.1 0.0 copy-start.7
  26.1 9.2 %shard_map.74.tiles_ref = bf16[72,32,128]{2,1,0:T(8,128)(2,1)S(1)} custom-call(s32[7,32]{1,0:T(8,128)S(1)} %bitcast.6, s32[7,4,32]{2,1,0:T(4,128)S(1)} %bitcast.5, s32[4,8,32]{2,1,0:T(8,128)S(1)} %bitcast.4, bf16[32,64,448]{2,1,0:T(8,128)(2,1)S(1)} %copy-done.2, bf16[32,64,256]{2,1,0:T(8,128)(2,1)S(1)} %copy-done.1, bf16[80,128,128]{2,1,0:T(8,128)(2,1)S(1)} %shard_map.73.x_ref), custom_call_target="tpu_custom_call" | custom-call | tf_op jit(solution)/shard_map/pallas_call | solution.py:248
  35.4 13.1 %shard_map.75.returned_ref = bf16[36,64,128]{2,1,0:T(8,128)(2,1)S(1)} custom-call(bf16[72,32,128]{2,1,0:T(8,128)(2,1)S(1)} %shard_map.74.tiles_ref), custom_call_target="tpu_custom_call" | custom-call | tf_op jit(solution)/shard_map/pallas_call | solution.py:264
  48.6 0.0 copy-done.7
  48.6 5.0 %shard_map.76 = f32[64,8192]{1,0:T(8,128)} custom-call(s32[1,72]{1,0:T(1,128)S(1)} %copy-done.7, bf16[36,64,128]{2,1,0:T(8,128)(2,1)S(1)} %shard_map.75.returned_ref), custom_call_target="tpu_custom_call" | custom-call | tf_op jit(solution)/shard_map/pallas_call | solution.py:276
Async XLA Ops:
  0.0 26.1 %copy-start.5 = (s32[32,7]{0,1:T(8,128)S(1)}, s32[32,7]{0,1:T(8,128)}, u32[]{:S(2)}) copy-start(s32[32,7]{0,1:T(8,128)} %param.9) | copy-start | bytes 2692
  0.0 1.2 %copy-start = (bf16[32,64,256]{2,1,0:T(8,128)(2,1)S(1)}, bf16[32,64,256]{2,1,0:T(8,128)(2,1)}, u32[]{:S(2)}) copy-start(bf16[32,64,256]{2,1,0:T(8,128)(2,1)} %p_ref.3) | copy-start | bytes 3145732
  1.2 0.7 %copy-start.6 = (s32[1,8,6]{1,0,2:T(1,128)S(1)}, s32[1,8,6]{1,0,2:T(1,128)}, u32[]{:S(2)}) copy-start(s32[1,8,6]{1,0,2:T(1,128)} %param.12) | copy-start | bytes 580
  1.9 24.2 %copy-start.1 = (bf16[32,64,256]{2,1,0:T(8,128)(2,1)S(1)}, bf16[32,64,256]{2,1,0:T(8,128)(2,1)}, u32[]{:S(2)}) copy-start(bf16[32,64,256]{2,1,0:T(8,128)(2,1)} %p_ref.3) | copy-start | bytes 3145732
  1.9 24.2 %copy-start.2 = (bf16[32,64,448]{2,1,0:T(8,128)(2,1)S(1)}, bf16[32,64,448]{2,1,0:T(8,128)(2,1)}, u32[]{:S(2)}) copy-start(bf16[32,64,448]{2,1,0:T(8,128)(2,1)} %a_ref.1) | copy-start | bytes 5505028
  1.9 24.2 %copy-start.3 = (s32[32,4,8]{0,2,1:T(8,128)S(1)}, s32[32,4,8]{0,2,1:T(8,128)}, u32[]{:S(2)}) copy-start(s32[32,4,8]{0,2,1:T(8,128)} %param.11) | copy-start | bytes 12292
  1.9 24.2 %copy-start.4 = (s32[32,7,4]{0,2,1:T(4,128)S(1)}, s32[32,7,4]{0,2,1:T(4,128)}, u32[]{:S(2)}) copy-start(s32[32,7,4]{0,2,1:T(4,128)} %param.10) | copy-start | bytes 10756
  26.1 22.4 %copy-start.7 = (s32[1,72]{1,0:T(1,128)S(1)}, s32[1,72]{1,0:T(1,128)}, u32[]{:S(2)}) copy-start(s32[1,72]{1,0:T(1,128)} %owner_map.1) | copy-start | bytes 868
